TPU v7x, 32 devices: a whole 2x2x4 slice. The times are simulated.
32 devices in a mesh: dp: 8 (over y, x, core), head: 4 (over z).
Axes of the slice: x: 2, y: 2, z: 4, core: 2. Of those that a mesh axis runs over, the one named last changes fastest.
Arguments:
- tokens: bfloat16 [16384, 1024], P(('dp', 'head')), may hold values from -6 to 6
- first_values: bfloat16 [16384, 1024], P('dp', 'head'), may hold values from -6 to 6
- mixer_in: float32 [3, 1024, 1024], P(None, 'dp', 'head'), may hold values from -0.1875 to 0.1875
- mixer_out: float32 [1024, 1024], P('head', 'dp'), may hold values from -0.75 to 0.75
- gate_up: float32 [2, 1024, 2816], P(None, 'dp', 'head'), may hold values from -0.1875 to 0.1875
- down_weight: float32 [2816, 1024], P('head', 'dp'), may hold values from -0.109375 to 0.109375
- norm_gains: float32 [2, 1024], P(None, 'dp'), may hold values from 0.5 to 1.5
- lengths: int32 [8], P('dp'), may hold values from 128 to 2048, as said below
- cotangent: bfloat16 [16384, 1024], P(('dp', 'head')), may hold values from -6 to 6
Outputs:
- block_out: bfloat16 [16384, 1024], P(('dp', 'head'))
- tokens_grad: float32 [16384, 1024], P(('dp', 'head'))
- first_grad: float32 [16384, 1024], P('dp', 'head')
- mixer_in_grad: float32 [3, 1024, 1024], P(None, 'dp', 'head')
- mixer_out_grad: float32 [1024, 1024], P('head', 'dp')
- gate_up_grad: float32 [2, 1024, 2816], P(None, 'dp', 'head')
- down_grad: float32 [2816, 1024], P('head', 'dp')
- gains_grad: float32 [2, 1024], P(None, 'dp')
Inputs may be any that keep to these rules, and one draw needn't show every extreme that they name: `lengths`: positions from a sequence's length on are padding; some sequence has exactly 2048 real tokens in every draw.
All inputs are finite; a program needn't handle non-finite values.
Results may differ from a plain program's by a relative error of at most 0.013.
The roundings to bfloat16 on the way count: a program that leaves them out, or rounds other values in their place, can miss the bound.
Values may be sent and summed in bfloat16 or wider, within the bound.
No kernel may reach another device: no remote copies, remote signals or barrier semaphores. Data moves between devices by JAX's collectives and lax.ppermute only.
A program may use at most 128 MiB of HBM per device.

v0:
```python
import jax
import jax.numpy as jnp
from jax import lax
from jax.sharding import PartitionSpec as P

HDIM = 64
SEQ = 2048
epsilon = 1e-05
far_below = -1e30
rope_base = 10000.0


def rope_tables(width):
    half = width // 2
    rates = rope_base ** (-jnp.arange(half, dtype=jnp.float32) * 2.0 / width)
    angles = jnp.arange(SEQ, dtype=jnp.float32)[:, None] * rates[None, :]
    return (jnp.cos(angles)[:, None, :], jnp.sin(angles)[:, None, :])


def rotate(field, cosine, sine, direction):
    half = field.shape[-1] // 2
    first = field[..., :half]
    second = field[..., half:]
    return jnp.concatenate(
        [first * cosine - direction * second * sine, second * cosine + direction * first * sine],
        axis=-1,
    )


def rms_parts(field, gain):
    factor = lax.rsqrt(jnp.mean(field * field, axis=-1, keepdims=True) + epsilon)
    unit = field * factor
    return (unit * gain, unit, factor)


def rms_back(normed_grad, unit, factor, gain):
    scaled = normed_grad * gain
    field_grad = factor * (scaled - unit * jnp.mean(scaled * unit, axis=-1, keepdims=True))
    return (field_grad, jnp.sum(normed_grad * unit, axis=0))


def to_items(rows, seqs_here, heads_here):
    return (
        rows.reshape(seqs_here, SEQ, heads_here, HDIM)
        .transpose(0, 2, 1, 3)
        .reshape(seqs_here * heads_here, SEQ, HDIM)
    )


def from_items(items, seqs_here, heads_here):
    return (
        items.reshape(seqs_here, heads_here, SEQ, HDIM)
        .transpose(0, 2, 1, 3)
        .reshape(seqs_here * SEQ, heads_here * HDIM)
    )


def block_scores(query_block, keys, rows, length):
    places = jnp.arange(SEQ)
    raw = jnp.einsum("qe,ke->qk", query_block, keys, preferred_element_type=jnp.float32)
    allowed = (places[None, :] <= rows[:, None]) & (places[None, :] < length)
    return jnp.where(allowed, raw * HDIM ** (-0.5), far_below)


def attend_item(item):
    query, keys, values, length = item
    block = min(512, SEQ)

    def one_block(number):
        start = number * block
        query_block = lax.dynamic_slice_in_dim(query, start, block, 0)
        rows = start + jnp.arange(block)
        scores = block_scores(query_block, keys, rows, length)
        peak = jnp.max(scores, axis=-1, keepdims=True)
        powers = jnp.exp(scores - peak)
        total = jnp.sum(powers, axis=-1, keepdims=True)
        probs = (powers / total).astype(jnp.bfloat16)
        result = (
            jnp.dot(probs, values, preferred_element_type=jnp.float32) * (rows < length)[:, None]
        )
        return (result.astype(jnp.bfloat16), (peak + jnp.log(total))[:, 0])

    results, log_total = lax.map(one_block, jnp.arange(SEQ // block))
    return (results.reshape(SEQ, HDIM), log_total.reshape(SEQ))


def attend_back(item):
    query, keys, values, length, log_total, out_grad = item
    block = min(512, SEQ)

    def one_block(carry, number):
        keys_grad, values_grad = carry
        start = number * block
        query_block = lax.dynamic_slice_in_dim(query, start, block, 0)
        grad_block = lax.dynamic_slice_in_dim(out_grad, start, block, 0)
        total_block = lax.dynamic_slice_in_dim(log_total, start, block, 0)
        rows = start + jnp.arange(block)
        scores = block_scores(query_block, keys, rows, length)
        probs = jnp.exp(scores - total_block[:, None])
        values_grad = values_grad + jnp.einsum(
            "qk,qe->ke", probs.astype(jnp.bfloat16), grad_block, preferred_element_type=jnp.float32
        )
        prob_grad = jnp.einsum("qe,ke->qk", grad_block, values, preferred_element_type=jnp.float32)
        offset = jnp.sum(prob_grad * probs, axis=-1, keepdims=True)
        raw_grad = (probs * (prob_grad - offset) * HDIM ** (-0.5)).astype(jnp.bfloat16)
        query_grad = jnp.dot(raw_grad, keys, preferred_element_type=jnp.float32)
        keys_grad = keys_grad + jnp.einsum(
            "qk,qe->ke", raw_grad, query_block, preferred_element_type=jnp.float32
        )
        return ((keys_grad, values_grad), query_grad)

    empty = jnp.zeros((SEQ, HDIM), jnp.float32)
    (keys_grad, values_grad), query_grads = lax.scan(
        one_block, (empty, empty), jnp.arange(SEQ // block)
    )
    return (query_grads.reshape(SEQ, HDIM), keys_grad, values_grad)


def shards(
    tokens, first_values, mixer_in, mixer_out, gate_up, down_weight, norm_gains, lengths, cotangent
):
    seqs_here = lengths.shape[0]
    group_rows = seqs_here * SEQ
    heads_here = mixer_in.shape[2] // HDIM
    cosine, sine = rope_tables(HDIM)
    places = jnp.arange(SEQ)
    valid_rows = (places[None, :] < lengths[:, None]).astype(jnp.float32).reshape(group_rows)
    head_lengths = jnp.repeat(lengths, heads_here)
    qkv_low = mixer_in.astype(jnp.bfloat16)
    proj_low = mixer_out.astype(jnp.bfloat16)
    gates_low = gate_up.astype(jnp.bfloat16)
    down_low = down_weight.astype(jnp.bfloat16)
    gain_low = norm_gains.astype(jnp.bfloat16)
    full = (
        lax.all_gather(qkv_low, "dp", axis=1, tiled=True),
        lax.all_gather(proj_low, "dp", axis=1, tiled=True),
        lax.all_gather(gates_low, "dp", axis=1, tiled=True),
        lax.all_gather(down_low, "dp", axis=1, tiled=True),
        lax.all_gather(gain_low, "dp", axis=1, tiled=True),
    )
    qkv_full, proj_full, gates_full, down_full, gain_full = full
    gain_first = gain_full[0].astype(jnp.float32)
    gain_second = gain_full[1].astype(jnp.float32)
    token_rows = tokens.astype(jnp.float32)
    normed_a, unit_a, factor_a = rms_parts(token_rows, gain_first)
    mixer_rows = lax.all_gather(normed_a.astype(jnp.bfloat16), "head", axis=0, tiled=True)
    mixed = jnp.einsum("td,kdc->ktc", mixer_rows, qkv_full, preferred_element_type=jnp.float32)
    shape_four = (seqs_here, SEQ, heads_here, HDIM)
    query = rotate(mixed[0].reshape(shape_four), cosine, sine, 1.0).astype(jnp.bfloat16)
    keys = rotate(mixed[1].reshape(shape_four), cosine, sine, 1.0).astype(jnp.bfloat16)
    values = (0.5 * mixed[2] + 0.5 * first_values.astype(jnp.float32)).astype(jnp.bfloat16)
    query_items = query.transpose(0, 2, 1, 3).reshape(seqs_here * heads_here, SEQ, HDIM)
    keys_items = keys.transpose(0, 2, 1, 3).reshape(seqs_here * heads_here, SEQ, HDIM)
    values_items = to_items(values, seqs_here, heads_here)
    attended_items, log_total = lax.map(
        attend_item, (query_items, keys_items, values_items, head_lengths)
    )
    attended = from_items(attended_items, seqs_here, heads_here)
    piece = attended
    branch_a = lax.psum_scatter(
        jnp.dot(piece, proj_full, preferred_element_type=jnp.float32),
        "head",
        scatter_dimension=0,
        tiled=True,
    )
    hidden_state = token_rows + branch_a
    normed_b, unit_b, factor_b = rms_parts(hidden_state, gain_second)
    feed_rows = lax.all_gather(normed_b.astype(jnp.bfloat16), "head", axis=0, tiled=True)
    gated = jnp.einsum("td,kdf->ktf", feed_rows, gates_full, preferred_element_type=jnp.float32)
    gate = gated[0]
    upward = gated[1]
    sigmoid_gate = jax.nn.sigmoid(gate)
    silu_gate = gate * sigmoid_gate
    inner = (silu_gate * upward).astype(jnp.bfloat16)
    piece = inner
    branch_b = lax.psum_scatter(
        jnp.dot(piece, down_full, preferred_element_type=jnp.float32).astype(jnp.bfloat16),
        "head",
        scatter_dimension=0,
        tiled=True,
    ).astype(jnp.float32)
    block_out = (hidden_state + branch_b).astype(jnp.bfloat16)
    back_full = (
        lax.all_gather(qkv_low, "dp", axis=1, tiled=True),
        lax.all_gather(proj_low, "dp", axis=1, tiled=True),
        lax.all_gather(gates_low, "dp", axis=1, tiled=True),
        lax.all_gather(down_low, "dp", axis=1, tiled=True),
        lax.all_gather(gain_low, "dp", axis=1, tiled=True),
    )
    qkv_back, proj_back, gates_back, down_back, gain_back = back_full
    piece = lax.all_gather(cotangent, "head", axis=0, tiled=True)
    down_sum = jnp.einsum("tf,td->fd", inner, piece, preferred_element_type=jnp.float32)
    rows_grad = jnp.einsum("td,fd->tf", piece, down_back, preferred_element_type=jnp.float32)
    inner_grad = rows_grad
    gate_grad = inner_grad * upward * sigmoid_gate * (1.0 + gate * (1.0 - sigmoid_gate))
    mlp_grad = jnp.stack([gate_grad, inner_grad * silu_gate]).astype(jnp.bfloat16)
    gates_part = jnp.einsum("td,ktf->kdf", feed_rows, mlp_grad, preferred_element_type=jnp.float32)
    piece = mlp_grad
    normed_b_grad = lax.psum_scatter(
        jnp.einsum("ktf,kdf->td", piece, gates_back, preferred_element_type=jnp.float32),
        "head",
        scatter_dimension=0,
        tiled=True,
    )
    state_part, gain_b_grad = rms_back(
        normed_b_grad, unit_b, factor_b, gain_back[1].astype(jnp.float32)
    )
    state_grad = cotangent.astype(jnp.float32) + state_part
    branch_grad = state_grad.astype(jnp.bfloat16)
    piece = lax.all_gather(branch_grad, "head", axis=0, tiled=True)
    proj_sum = jnp.einsum("tc,td->cd", attended, piece, preferred_element_type=jnp.float32)
    rows_grad = jnp.einsum("td,cd->tc", piece, proj_back, preferred_element_type=jnp.float32)
    attended_grad = rows_grad
    attended_grad = (valid_rows[:, None] * attended_grad).astype(jnp.bfloat16)
    grad_items = to_items(attended_grad, seqs_here, heads_here)
    query_grad, keys_grad, values_grad = lax.map(
        attend_back, (query_items, keys_items, values_items, head_lengths, log_total, grad_items)
    )
    values_mix_grad = from_items(values_grad, seqs_here, heads_here)
    first_grad = 0.5 * values_mix_grad
    query_rows = query_grad.reshape(seqs_here, heads_here, SEQ, HDIM).transpose(0, 2, 1, 3)
    keys_rows = keys_grad.reshape(seqs_here, heads_here, SEQ, HDIM).transpose(0, 2, 1, 3)
    query_back = rotate(query_rows, cosine, sine, -1.0).reshape(group_rows, heads_here * HDIM)
    keys_back = rotate(keys_rows, cosine, sine, -1.0).reshape(group_rows, heads_here * HDIM)
    mixed_grad = jnp.stack([query_back, keys_back, 0.5 * values_mix_grad]).astype(jnp.bfloat16)
    qkv_part = jnp.einsum("td,ktc->kdc", mixer_rows, mixed_grad, preferred_element_type=jnp.float32)
    piece = mixed_grad
    normed_a_grad = lax.psum_scatter(
        jnp.einsum("ktc,kdc->td", piece, qkv_back, preferred_element_type=jnp.float32).astype(
            jnp.bfloat16
        ),
        "head",
        scatter_dimension=0,
        tiled=True,
    ).astype(jnp.float32)
    token_part, gain_a_grad = rms_back(
        normed_a_grad, unit_a, factor_a, gain_back[0].astype(jnp.float32)
    )
    tokens_grad = state_grad + token_part
    gain_grads = jnp.stack([gain_a_grad, gain_b_grad])
    summed = (
        lax.psum_scatter(qkv_part, "dp", scatter_dimension=1, tiled=True),
        lax.psum_scatter(proj_sum, "dp", scatter_dimension=1, tiled=True),
        lax.psum_scatter(gates_part, "dp", scatter_dimension=1, tiled=True),
        lax.psum_scatter(down_sum, "dp", scatter_dimension=1, tiled=True),
        lax.psum_scatter(gain_grads, "dp", scatter_dimension=1, tiled=True),
    )
    gains_grad = lax.psum(summed[4], "head")
    return (
        block_out,
        tokens_grad,
        first_grad,
        summed[0],
        summed[1],
        summed[2],
        summed[3],
        gains_grad,
    )


def solution(mesh):
    return jax.shard_map(
        shards,
        mesh=mesh,
        in_specs=(
            P(("dp", "head"), None),
            P("dp", "head"),
            P(None, "dp", "head"),
            P("head", "dp"),
            P(None, "dp", "head"),
            P("head", "dp"),
            P(None, "dp"),
            P("dp"),
            P(("dp", "head"), None),
        ),
        out_specs=(
            P(("dp", "head"), None),
            P(("dp", "head"), None),
            P("dp", "head"),
            P(None, "dp", "head"),
            P("head", "dp"),
            P(None, "dp", "head"),
            P("head", "dp"),
            P(None, "dp"),
        ),
        check_vma=False,
    )
```

profile of v0, /device:TPU:0, one launch (start us, length us, event | category | flops | bytes accessed | tf_op | source)
XLA Modules:
  0.0 1471.1 jit_solution(9712456741320512277)
XLA Ops:
  39.8 83.2 %all-gather.8.cloned.1.call-done = bf16[2048,1024]{1,0:T(8,128)(2,1)} async-done(((bf16[512,1024]{1,0:T(8,128)(2,1)}), bf16[2048,1024]{1,0:T(8,128)(2,1)}) %all-gather.8.cloned.1.call-update) | async-done | bytes 4194320 | tf_op jit(solution)/shard_map/all_gather | solution.py:146
  135.0 127.7 %while.54 = (s32[]{:T(128)}, bf16[4,2048,64]{1,2,0:T(8,128)(2,1)}, f32[4,2048]{1,0:T(4,128)S(1)}, bf16[4,2048,64]{2,1,0:T(8,128)(2,1)}, bf16[4,2048,64]{2,1,0:T(...) while((s32[]{:T(128)}, bf16[4,2048,64]{1,2,0:T(8,128)(2,1)}, ...), condition=%wide.region_6.7_spmd, body=%wide.region_1.6_spmd.sunk | while | flops 278990336 | bytes 16777708 | solution.py:155
  138.6 27.0 %while.57 = (s32[]{:T(128)}, bf16[4,512,64]{1,2,0:T(8,128)(2,1)S(1)}, f32[4,512]{1,0:T(4,128)S(1)}, s32[4]{0:T(128)S(1)}, s32[]{:T(128)}, /*index=5*/bf16[2048,6...) while((s32[]{:T(128)}, ...), condition=%wide.region_5.5_spmd, body=%wide.region_2.4_spmd.sunk | while | flops 278990336 | bytes 13598931 | solution.py:83
  170.5 27.0 %while.57 = (s32[]{:T(128)}, bf16[4,512,64]{1,2,0:T(8,128)(2,1)S(1)}, f32[4,512]{1,0:T(4,128)S(1)}, s32[4]{0:T(128)S(1)}, s32[]{:T(128)}, /*index=5*/bf16[2048,6...) while((s32[]{:T(128)}, ...), condition=%wide.region_5.5_spmd, body=%wide.region_2.4_spmd.sunk | while | flops 278990336 | bytes 13598931 | solution.py:83
  202.4 27.0 %while.57 = (s32[]{:T(128)}, bf16[4,512,64]{1,2,0:T(8,128)(2,1)S(1)}, f32[4,512]{1,0:T(4,128)S(1)}, s32[4]{0:T(128)S(1)}, s32[]{:T(128)}, /*index=5*/bf16[2048,6...) while((s32[]{:T(128)}, ...), condition=%wide.region_5.5_spmd, body=%wide.region_2.4_spmd.sunk | while | flops 278990336 | bytes 13598931 | solution.py:83
  234.3 27.0 %while.57 = (s32[]{:T(128)}, bf16[4,512,64]{1,2,0:T(8,128)(2,1)S(1)}, f32[4,512]{1,0:T(4,128)S(1)}, s32[4]{0:T(128)S(1)}, s32[]{:T(128)}, /*index=5*/bf16[2048,6...) while((s32[]{:T(128)}, ...), condition=%wide.region_5.5_spmd, body=%wide.region_2.4_spmd.sunk | while | flops 278990336 | bytes 13598931 | solution.py:83
  271.4 141.2 %reduce-scatter.12.cloned.1.call-done = f32[512,1024]{1,0:T(8,128)} async-done(((f32[2048,1024]{1,0:T(8,128)}), f32[512,1024]{1,0:T(8,128)}) %reduce-scatter.12.cloned.1.call-update) | async-done | bytes 2097168 | tf_op jit(solution)/shard_map/reduce_scatter | solution.py:160
  417.9 29.4 %all-gather.14.cloned.1.call-done = bf16[2,1024,704]{1,2,0:T(8,128)(2,1)} async-done(((bf16[2,128,704]{1,2,0:T(8,128)(2,1)}), bf16[2,1024,704]{1,2,0:T(8,128)(2,1)}) %all-gather.14.cloned.1.call-update) | async-done | bytes 2883600 | tf_op jit(solution)/shard_map/all_gather | solution.py:137
  447.3 82.8 %all-gather.12.cloned.1.call-done = bf16[2048,1024]{1,0:T(8,128)(2,1)} async-done(((bf16[512,1024]{1,0:T(8,128)(2,1)}), bf16[2048,1024]{1,0:T(8,128)(2,1)}) %all-gather.12.cloned.1.call-update) | async-done | bytes 4194320 | tf_op jit(solution)/shard_map/all_gather | solution.py:168
  556.2 82.4 %all-gather.18.cloned.1.call-done = bf16[2048,1024]{1,0:T(8,128)(2,1)} async-done(((bf16[512,1024]{1,0:T(8,128)(2,1)}), bf16[2048,1024]{1,0:T(8,128)(2,1)}) %all-gather.18.cloned.1.call-update) | async-done | bytes 4194320 | tf_op jit(solution)/shard_map/all_gather | solution.py:191
  661.5 143.1 %reduce-scatter.16.cloned.1.call-done = f32[512,1024]{1,0:T(8,128)} async-done(((f32[2048,1024]{1,0:T(8,128)}), f32[512,1024]{1,0:T(8,128)}) %reduce-scatter.16.cloned.1.call-update) | async-done | bytes 2097168 | tf_op jit(solution)/shard_map/reduce_scatter | solution.py:199
  809.5 81.4 %all-gather.20.cloned.1.call-done = bf16[2048,1024]{1,0:T(8,128)(2,1)} async-done(((bf16[512,1024]{1,0:T(8,128)(2,1)}), bf16[2048,1024]{1,0:T(8,128)(2,1)}) %all-gather.20.cloned.1.call-update) | async-done | bytes 4194320 | tf_op jit(solution)/shard_map/all_gather | solution.py:210
  896.3 154.4 %while.56 = (s32[]{:T(128)}, f32[4,2048,64]{1,2,0:T(8,128)}, f32[4,2048,64]{1,2,0:T(8,128)}, f32[4,2048,64]{1,2,0:T(8,128)}, bf16[4,2048,64]{2,1,0:T(8,128)(2,1)...) while((s32[]{:T(128)}, f32[4,2048,64]{1,2,0:T(8,128)}, ...), condition=%wide.region_16.17_spmd, body=%wide.region_12.16_spmd.sunk | while | flops 684197888 | bytes 42895948 | solution.py:216
  901.3 30.0 %while.58 = (s32[]{:T(128)}, f32[2048,64]{0,1:T(8,128)S(1)}, f32[2048,64]{0,1:T(8,128)S(1)}, f32[4,512,64]{1,2,0:T(8,128)}, s32[4]{0:T(128)S(1)}, /*index=5*/s32...) while((s32[]{:T(128)}, f32[2048,64]{0,1:T(8,128)S(1)}, ...), condition=%wide.region_15.15_spmd.clone, body=%wide.region_13.14_spmd.clone.sunk | while | flops 684197888 | bytes 35539192 | solution.py:113
  939.9 30.0 %while.58 = (s32[]{:T(128)}, f32[2048,64]{0,1:T(8,128)S(1)}, f32[2048,64]{0,1:T(8,128)S(1)}, f32[4,512,64]{1,2,0:T(8,128)}, s32[4]{0:T(128)S(1)}, /*index=5*/s32...) while((s32[]{:T(128)}, f32[2048,64]{0,1:T(8,128)S(1)}, ...), condition=%wide.region_15.15_spmd.clone, body=%wide.region_13.14_spmd.clone.sunk | while | flops 684197888 | bytes 35539192 | solution.py:113
  978.5 30.0 %while.58 = (s32[]{:T(128)}, f32[2048,64]{0,1:T(8,128)S(1)}, f32[2048,64]{0,1:T(8,128)S(1)}, f32[4,512,64]{1,2,0:T(8,128)}, s32[4]{0:T(128)S(1)}, /*index=5*/s32...) while((s32[]{:T(128)}, f32[2048,64]{0,1:T(8,128)S(1)}, ...), condition=%wide.region_15.15_spmd.clone, body=%wide.region_13.14_spmd.clone.sunk | while | flops 684197888 | bytes 35539192 | solution.py:113
  1017.1 30.0 %while.58 = (s32[]{:T(128)}, f32[2048,64]{0,1:T(8,128)S(1)}, f32[2048,64]{0,1:T(8,128)S(1)}, f32[4,512,64]{1,2,0:T(8,128)}, s32[4]{0:T(128)S(1)}, /*index=5*/s32...) while((s32[]{:T(128)}, f32[2048,64]{0,1:T(8,128)S(1)}, ...), condition=%wide.region_15.15_spmd.clone, body=%wide.region_13.14_spmd.clone.sunk | while | flops 684197888 | bytes 35539192 | solution.py:113
  1086.5 58.5 %reduce-scatter.18.cloned.1.call-done = bf16[512,1024]{1,0:T(8,128)(2,1)} async-done(((bf16[2048,1024]{1,0:T(8,128)(2,1)}), bf16[512,1024]{1,0:T(8,128)(2,1)}) %reduce-scatter.18.cloned.1.call-update) | async-done | bytes 1048592 | tf_op jit(solution)/shard_map/reduce_scatter | solution.py:228
  1176.2 19.3 %reduce-scatter.20.cloned.1.call-done = f32[3,128,256]{1,2,0:T(8,128)} async-done(((f32[3,1024,256]{1,2,0:T(8,128)}), f32[3,128,256]{1,2,0:T(8,128)}) %reduce-scatter.20.cloned.1.call-update) | async-done | bytes 393232 | tf_op jit(solution)/shard_map/reduce_scatter | solution.py:242
  1197.4 77.0 %reduce-scatter.14.cloned.1.call-done = bf16[512,1024]{1,0:T(8,128)(2,1)} async-done(((bf16[2048,1024]{1,0:T(8,128)(2,1)}), bf16[512,1024]{1,0:T(8,128)(2,1)}) %reduce-scatter.14.cloned.1.call-update) | async-done | bytes 1048592 | tf_op jit(solution)/shard_map/reduce_scatter | solution.py:176
  1278.7 33.8 %reduce-scatter.28.cloned.1.call-done = f32[128,2]{1,0:T(8,128)} async-done(((f32[1024,2]{1,0:T(8,128)}), f32[128,2]{1,0:T(8,128)}) %reduce-scatter.28.cloned.1.call-update) | async-done | bytes 1040
  1325.6 35.6 %reduce-scatter.26.cloned.1.call-done = f32[704,128]{1,0:T(8,128)} async-done(((f32[704,1024]{1,0:T(8,128)}), f32[704,128]{1,0:T(8,128)}) %reduce-scatter.26.cloned.1.call-update) | async-done | bytes 360464 | tf_op jit(solution)/shard_map/reduce_scatter | solution.py:245
  1361.2 63.3 %reduce-scatter.24.cloned.1.call-done = f32[2,128,704]{1,2,0:T(8,128)} async-done(((f32[2,1024,704]{1,2,0:T(8,128)}), f32[2,128,704]{1,2,0:T(8,128)}) %reduce-scatter.24.cloned.1.call-update) | async-done | bytes 720912 | tf_op jit(solution)/shard_map/reduce_scatter | solution.py:244
  1424.5 39.6 %reduce-scatter.22.cloned.1.call-done = f32[256,128]{1,0:T(8,128)} async-done(((f32[256,1024]{1,0:T(8,128)}), f32[256,128]{1,0:T(8,128)}) %reduce-scatter.22.cloned.1.call-update) | async-done | bytes 131088 | tf_op jit(solution)/shard_map/reduce_scatter | solution.py:243
  (569 shorter events, 462.6 us)
Async XLA Ops:
  7.2 32.6 %all-gather.10.cloned.1.call-start = ((), (), s32[]{:S(2)}) async-start(), calls=%async_computation.10 | async-start | bytes 1769472 | tf_op jit(solution)/shard_map/all_gather | solution.py:135
  9.1 113.8 %all-gather.8.cloned.1.call-start = ((), (), s32[]{:S(2)}) async-start(), calls=%async_computation.9 | async-start | bytes 5242880 | tf_op jit(solution)/shard_map/all_gather | solution.py:146
  23.6 389.0 %reduce-scatter.12.cloned.1.call-start = ((), (), s32[]{:S(2)}) async-start(), calls=%async_computation.11 | async-start | bytes 10485760 | tf_op jit(solution)/shard_map/reduce_scatter | solution.py:160
  269.4 143.2 %copy-start.3 = (bf16[512,1024]{1,0:T(8,128)(2,1)S(1)}, bf16[512,1024]{1,0:T(8,128)(2,1)}, u32[]{:S(2)}) copy-start(bf16[512,1024]{1,0:T(8,128)(2,1)} %param.17) | copy-start | bytes 3145732
  269.4 177.9 %all-gather.14.cloned.1.call-start = ((), (), s32[]{:S(2)}) async-start(), calls=%async_computation.13 | async-start | bytes 3244032 | tf_op jit(solution)/shard_map/all_gather | solution.py:137
  271.3 143.2 %copy-start.19 = (f32[1,1024]{1,0:T(1,128)S(1)}, f32[1,1024]{1,0:T(1,128)}, u32[]{:S(2)}) copy-start(f32[1,1024]{1,0:T(1,128)} %get-tuple-element.425) | copy-start | bytes 12292
  271.3 258.8 %all-gather.12.cloned.1.call-start = ((), (), s32[]{:S(2)}) async-start(), calls=%async_computation.12 | async-start | bytes 5242880 | tf_op jit(solution)/shard_map/all_gather | solution.py:168
  414.5 393.0 %copy-start = (f32[512,1024]{1,0:T(8,128)}, f32[512,1024]{1,0:T(8,128)S(1)}, u32[]{:S(2)}) copy-start(f32[512,1024]{1,0:T(8,128)S(1)} %get-tuple-element.395) | copy-start | bytes 6291460
  414.5 393.0 %copy-start.23 = (f32[512]{0:T(512)}, f32[512]{0:T(512)S(1)}, u32[]{:S(2)}) copy-start(f32[512]{0:T(512)S(1)} %add_rsqrt_fusion) | copy-start | bytes 6148
  415.8 140.4 %all-gather.16.cloned.1.call-start = ((), (), s32[]{:S(2)}) async-start(), calls=%async_computation.14 | async-start | bytes 1622016 | tf_op jit(solution)/shard_map/all_gather | solution.py:138
  416.6 222.0 %all-gather.18.cloned.1.call-start = ((), (), s32[]{:S(2)}) async-start(), calls=%async_computation.16 | async-start | bytes 5242880 | tf_op jit(solution)/shard_map/all_gather | solution.py:191
  417.3 387.3 %reduce-scatter.16.cloned.1.call-start = ((), (), s32[]{:S(2)}) async-start(), calls=%async_computation.17 | async-start | bytes 10485760 | tf_op jit(solution)/shard_map/reduce_scatter | solution.py:199
  661.5 146.1 %copy-start.7 = (bf16[512,1024]{1,0:T(8,128)(2,1)S(1)}, bf16[512,1024]{1,0:T(8,128)(2,1)}, u32[]{:S(2)}) copy-start(bf16[512,1024]{1,0:T(8,128)(2,1)} %param.25) | copy-start | bytes 3145732
  661.5 229.4 %all-gather.20.cloned.1.call-start = ((), (), s32[]{:S(2)}) async-start(), calls=%async_computation.18 | async-start | bytes 5242880 | tf_op jit(solution)/shard_map/all_gather | solution.py:210
  809.2 335.7 %reduce-scatter.18.cloned.1.call-start = ((), (), s32[]{:S(2)}) async-start(), calls=%async_computation.19 | async-start | bytes 5242880 | tf_op jit(solution)/shard_map/reduce_scatter | solution.py:228
  896.3 154.5 %copy-start.9 = (f32[2048,32]{0,1:T(8,128)S(1)}, f32[2048,32]{0,1:T(8,128)}, u32[]{:S(2)}) copy-start(f32[2048,32]{0,1:T(8,128)} %copy-done.8) | copy-start | bytes 786436
  1069.5 126.0 %reduce-scatter.20.cloned.1.call-start = ((), (), s32[]{:S(2)}) async-start(), calls=%async_computation.20 | async-start | bytes 3538944 | tf_op jit(solution)/shard_map/reduce_scatter | solution.py:242
  1078.2 196.3 %reduce-scatter.14.cloned.1.call-start = ((), (), s32[]{:S(2)}) async-start(), calls=%async_computation.15 | async-start | bytes 5242880 | tf_op jit(solution)/shard_map/reduce_scatter | solution.py:176
  1086.4 226.1 %reduce-scatter.28.cloned.1.call-start = ((), (), s32[]{:S(2)}) async-start(), calls=%async_computation.24 | async-start | bytes 589824
  1148.1 213.1 %reduce-scatter.26.cloned.1.call-start = ((), (), s32[]{:S(2)}) async-start(), calls=%async_computation.23 | async-start | bytes 3244032 | tf_op jit(solution)/shard_map/reduce_scatter | solution.py:245
  1155.9 268.6 %reduce-scatter.24.cloned.1.call-start = ((), (), s32[]{:S(2)}) async-start(), calls=%async_computation.22 | async-start | bytes 6488064 | tf_op jit(solution)/shard_map/reduce_scatter | solution.py:244
  1167.5 296.6 %reduce-scatter.22.cloned.1.call-start = ((), (), s32[]{:S(2)}) async-start(), calls=%async_computation.21 | async-start | bytes 1179648 | tf_op jit(solution)/shard_map/reduce_scatter | solution.py:243
  1173.2 101.3 %copy-start.1 = (f32[512,1024]{1,0:T(8,128)S(1)}, f32[512,1024]{1,0:T(8,128)}, u32[]{:S(2)}) copy-start(f32[512,1024]{1,0:T(8,128)} %copy-done) | copy-start | bytes 6291460
  1173.2 101.3 %copy-start.20 = (f32[1,1024]{1,0:T(1,128)S(1)}, f32[1,1024]{1,0:T(1,128)}, u32[]{:S(2)}) copy-start(f32[1,1024]{1,0:T(1,128)} %get-tuple-element.425) | copy-start | bytes 12292
  (26 other events, 599.1 us)
Sparse Core Ops, SparseCore 0:
  10.5 29.2 all-gather.9
  41.9 80.9 all-gather.7
  269.5 143.0 reduce-scatter.11
  414.9 32.3 all-gather.13
  449.3 80.7 all-gather.11
  532.4 23.8 all-gather.15
  557.8 80.7 all-gather.17
  661.6 143.0 reduce-scatter.15
  809.4 81.4 all-gather.19
  1069.6 75.2 reduce-scatter.17
  1148.7 46.7 reduce-scatter.19
  1197.7 76.7 reduce-scatter.13
  1277.8 34.6 reduce-scatter.27
  1316.3 44.8 reduce-scatter.25
  1365.5 58.9 reduce-scatter.23
  1428.1 35.9 reduce-scatter.21
where the time goes:
time: 1480 us; the launch traced here: 1470 us
  waiting for transfers between devices  987 us (67%)
  matrix products  226 us (15%)
  local copies, waits for them, and re-layouts  102 us (7%)
  other arithmetic  81.1 us (5%)
  blocking collectives  34.4 us (2%)
  loops' own time  22.6 us (2%)
  between operations  15.4 us (1%)
    reduce_scatter x1, waiting for transfers between devices, shards(): lax.psum_scatter(jnp.einsum('ktf,kdf->td', piece, gates_back, preferred_e...  143 us
    reduce_scatter x1, waiting for transfers between devices, shards(): lax.psum_scatter(jnp.dot(piece, proj_full, preferred_element_type=jnp.flo...  141 us
    all_gather x1, waiting for transfers between devices, shards(): lax.all_gather(normed_a.astype(jnp.bfloat16), 'head', axis=0, tiled=True)  83.2 us
    all_gather x1, waiting for transfers between devices, shards(): lax.all_gather(normed_b.astype(jnp.bfloat16), 'head', axis=0, tiled=True)  82.8 us
    all_gather x1, waiting for transfers between devices, shards(): piece = lax.all_gather(cotangent, 'head', axis=0, tiled=True)  82.4 us
    all_gather x1, waiting for transfers between devices, shards(): piece = lax.all_gather(branch_grad, 'head', axis=0, tiled=True)  81.4 us
    reduce_scatter x1, waiting for transfers between devices, shards(): lax.psum_scatter(jnp.dot(piece, down_full, preferred_element_type=jnp.flo...  77 us
    reduce_scatter x1, waiting for transfers between devices, shards(): lax.psum_scatter(gates_part, 'dp', scatter_dimension=1, tiled=True)  63.3 us
  transfers between devices with their start and end apart: 16, of which 16 were waited for; matrix products, arithmetic and copies ran while one was open for 5% of the time, Pallas kernels for 0%

commit v1 on v0

--- a/solution.py
+++ b/solution.py
@@ -188,7 +188,13 @@
         lax.all_gather(gain_low, "dp", axis=1, tiled=True),
     )
     qkv_back, proj_back, gates_back, down_back, gain_back = back_full
-    piece = lax.all_gather(cotangent, "head", axis=0, tiled=True)
+    n_dev = lax.axis_size("head")
+    held, blocks = (cotangent, [cotangent])
+    for _ in range(n_dev - 1):
+        held = lax.ppermute(held, "head", [(i, (i + 1) % n_dev) for i in range(n_dev)])
+        blocks.insert(0, held)
+    line = jnp.concatenate(blocks, axis=0)
+    piece = jnp.roll(line, (lax.axis_index("head") + 1) * cotangent.shape[0], axis=0)
     down_sum = jnp.einsum("tf,td->fd", inner, piece, preferred_element_type=jnp.float32)
     rows_grad = jnp.einsum("td,fd->tf", piece, down_back, preferred_element_type=jnp.float32)
     inner_grad = rows_grad

time: 1480 us -> 1430 us (0.966)
  waiting for transfers between devices: 987 us -> 908 us
  local copies, waits for them, and re-layouts: 102 us -> 117 us
    ppermute x0 -> x3, waiting for transfers between devices: none -> 104 us  [shards(): lax.ppermute(held, 'head', [(i, (i + 1) % n_dev) for i in range(n_dev)])]
    all_gather x1 -> x0, waiting for transfers between devices: 82.4 us -> none  [shards(): piece = lax.all_gather(cotangent, 'head', axis=0, tiled=True)]
    all_gather x1, waiting for transfers between devices: 82.8 us -> 14 us  [shards(): lax.all_gather(normed_b.astype(jnp.bfloat16), 'head', axis=0, tiled=True)]
    all_gather x1, waiting for transfers between devices: 29.4 us -> 0.01 us  [shards(): lax.all_gather(gates_low, 'dp', axis=1, tiled=True)]
    unnamed x74 -> x81, local copies, waits for them, and re-layouts: 16.9 us -> 31.1 us
    unnamed x17 -> x16, waiting for transfers between devices: 34.7 us -> 33.9 us
  transfers between devices with their start and end apart: 16 -> 18, of which waited for: 16 -> 16; matrix products, arithmetic and copies ran while one was open for 5% -> 6% of each run, Pallas kernels for 0% -> 0%
where the time goes in v1:
time: 1430 us; the launch traced here: 1420 us
  waiting for transfers between devices  908 us (63%)
  matrix products  227 us (16%)
  local copies, waits for them, and re-layouts  117 us (8%)
  other arithmetic  82 us (6%)
  blocking collectives  35.4 us (2%)
  loops' own time  21.9 us (2%)
  between operations  15.4 us (1%)
    reduce_scatter x1, waiting for transfers between devices, shards(): lax.psum_scatter(jnp.einsum('ktf,kdf->td', piece, gates_back, preferred_e...  145 us
    reduce_scatter x1, waiting for transfers between devices, shards(): lax.psum_scatter(jnp.dot(piece, proj_full, preferred_element_type=jnp.flo...  141 us
    ppermute x3, waiting for transfers between devices, shards(): lax.ppermute(held, 'head', [(i, (i + 1) % n_dev) for i in range(n_dev)])  104 us
    all_gather x1, waiting for transfers between devices, shards(): lax.all_gather(normed_a.astype(jnp.bfloat16), 'head', axis=0, tiled=True)  81.9 us
    all_gather x1, waiting for transfers between devices, shards(): piece = lax.all_gather(branch_grad, 'head', axis=0, tiled=True)  81.4 us
    reduce_scatter x1, waiting for transfers between devices, shards(): lax.psum_scatter(jnp.dot(piece, down_full, preferred_element_type=jnp.flo...  77.2 us
    reduce_scatter x1, waiting for transfers between devices, shards(): lax.psum_scatter(gates_part, 'dp', scatter_dimension=1, tiled=True)  63.3 us
    dot_general x32, matrix products, block_scores(): jnp.einsum('qe,ke->qk', query_block, keys, preferred_element_type=jnp.flo...  61.9 us
  transfers between devices with their start and end apart: 18, of which 16 were waited for; matrix products, arithmetic and copies ran while one was open for 6% of the time, Pallas kernels for 0%

profile of v1, /device:TPU:0, one launch (start us, length us, event | category | flops | bytes accessed | tf_op | source)
XLA Modules:
  0.0 1419.0 jit_solution(10024100544367169658)
XLA Ops:
  41.6 81.9 %all-gather.7.cloned.1.call-done = bf16[2048,1024]{1,0:T(8,128)(2,1)} async-done(((bf16[512,1024]{1,0:T(8,128)(2,1)}), bf16[2048,1024]{1,0:T(8,128)(2,1)}) %all-gather.7.cloned.1.call-update) | async-done | bytes 4194320 | tf_op jit(solution)/shard_map/all_gather | solution.py:146
  135.4 127.7 %while.54 = (s32[]{:T(128)}, bf16[4,2048,64]{1,2,0:T(8,128)(2,1)}, f32[4,2048]{1,0:T(4,128)S(1)}, bf16[4,2048,64]{2,1,0:T(8,128)(2,1)}, bf16[4,2048,64]{2,1,0:T(...) while((s32[]{:T(128)}, bf16[4,2048,64]{1,2,0:T(8,128)(2,1)}, ...), condition=%wide.region_6.7_spmd, body=%wide.region_1.6_spmd.sunk | while | flops 278990336 | bytes 16777708 | solution.py:155
  139.0 27.0 %while.57 = (s32[]{:T(128)}, bf16[4,512,64]{1,2,0:T(8,128)(2,1)S(1)}, f32[4,512]{1,0:T(4,128)S(1)}, s32[4]{0:T(128)S(1)}, s32[]{:T(128)}, /*index=5*/bf16[2048,6...) while((s32[]{:T(128)}, ...), condition=%wide.region_5.5_spmd, body=%wide.region_2.4_spmd.sunk | while | flops 278990336 | bytes 13598931 | solution.py:83
  170.9 27.0 %while.57 = (s32[]{:T(128)}, bf16[4,512,64]{1,2,0:T(8,128)(2,1)S(1)}, f32[4,512]{1,0:T(4,128)S(1)}, s32[4]{0:T(128)S(1)}, s32[]{:T(128)}, /*index=5*/bf16[2048,6...) while((s32[]{:T(128)}, ...), condition=%wide.region_5.5_spmd, body=%wide.region_2.4_spmd.sunk | while | flops 278990336 | bytes 13598931 | solution.py:83
  202.9 27.0 %while.57 = (s32[]{:T(128)}, bf16[4,512,64]{1,2,0:T(8,128)(2,1)S(1)}, f32[4,512]{1,0:T(4,128)S(1)}, s32[4]{0:T(128)S(1)}, s32[]{:T(128)}, /*index=5*/bf16[2048,6...) while((s32[]{:T(128)}, ...), condition=%wide.region_5.5_spmd, body=%wide.region_2.4_spmd.sunk | while | flops 278990336 | bytes 13598931 | solution.py:83
  234.8 27.0 %while.57 = (s32[]{:T(128)}, bf16[4,512,64]{1,2,0:T(8,128)(2,1)S(1)}, f32[4,512]{1,0:T(4,128)S(1)}, s32[4]{0:T(128)S(1)}, s32[]{:T(128)}, /*index=5*/bf16[2048,6...) while((s32[]{:T(128)}, ...), condition=%wide.region_5.5_spmd, body=%wide.region_2.4_spmd.sunk | while | flops 278990336 | bytes 13598931 | solution.py:83
  271.8 141.2 %reduce-scatter.12.cloned.1.call-done = f32[512,1024]{1,0:T(8,128)} async-done(((f32[2048,1024]{1,0:T(8,128)}), f32[512,1024]{1,0:T(8,128)}) %reduce-scatter.12.cloned.1.call-update) | async-done | bytes 2097168 | tf_op jit(solution)/shard_map/reduce_scatter | solution.py:160
  418.1 25.3 %collective-permute-done = bf16[512,1024]{1,0:T(8,128)(2,1)S(1)} collective-permute-done((bf16[512,1024]{1,0:T(8,128)(2,1)S(1)}, bf16[512,1024]{1,0:T(8,128)(2,1)S(1)}, u32[]{:S(2)}, u32[]{:S(2)}) %collective-permute-start) | collective-permute-done | bytes 1048608 | tf_op jit(solution)/shard_map/ppermute | solution.py:194
  445.0 36.1 %collective-permute-done.1 = bf16[512,1024]{1,0:T(8,128)(2,1)} collective-permute-done((bf16[512,1024]{1,0:T(8,128)(2,1)S(1)}, bf16[512,1024]{1,0:T(8,128)(2,1)}, u32[]{:S(2)}, u32[]{:S(2)}) %collective-permute-start.1) | collective-permute-done | bytes 1048608 | tf_op jit(solution)/shard_map/ppermute | solution.py:194
  491.6 42.1 %collective-permute-done.2 = bf16[512,1024]{1,0:T(8,128)(2,1)} collective-permute-done((bf16[512,1024]{1,0:T(8,128)(2,1)}, bf16[512,1024]{1,0:T(8,128)(2,1)}, u32[]{:S(2)}, u32[]{:S(2)}) %collective-permute-start.2) | collective-permute-done | bytes 1048608 | tf_op jit(solution)/shard_map/ppermute | solution.py:194
  609.9 144.6 %reduce-scatter.16.cloned.1.call-done = f32[512,1024]{1,0:T(8,128)} async-done(((f32[2048,1024]{1,0:T(8,128)}), f32[512,1024]{1,0:T(8,128)}) %reduce-scatter.16.cloned.1.call-update) | async-done | bytes 2097168 | tf_op jit(solution)/shard_map/reduce_scatter | solution.py:205
  759.3 81.4 %all-gather.17.cloned.1.call-done = bf16[2048,1024]{1,0:T(8,128)(2,1)} async-done(((bf16[512,1024]{1,0:T(8,128)(2,1)}), bf16[2048,1024]{1,0:T(8,128)(2,1)}) %all-gather.17.cloned.1.call-update) | async-done | bytes 4194320 | tf_op jit(solution)/shard_map/all_gather | solution.py:216
  846.1 153.7 %while.56 = (s32[]{:T(128)}, f32[4,2048,64]{1,2,0:T(8,128)}, f32[4,2048,64]{1,2,0:T(8,128)}, f32[4,2048,64]{1,2,0:T(8,128)}, bf16[4,2048,64]{2,1,0:T(8,128)(2,1)...) while((s32[]{:T(128)}, f32[4,2048,64]{1,2,0:T(8,128)}, ...), condition=%wide.region_16.17_spmd, body=%wide.region_12.16_spmd.sunk | while | flops 684197888 | bytes 42895948 | solution.py:222
  851.1 29.9 %while.58 = (s32[]{:T(128)}, f32[2048,64]{0,1:T(8,128)S(1)}, f32[2048,64]{0,1:T(8,128)S(1)}, f32[4,512,64]{1,2,0:T(8,128)}, s32[4]{0:T(128)S(1)}, /*index=5*/s32...) while((s32[]{:T(128)}, f32[2048,64]{0,1:T(8,128)S(1)}, ...), condition=%wide.region_15.15_spmd.clone, body=%wide.region_13.14_spmd.clone.sunk | while | flops 684197888 | bytes 35539192 | solution.py:113
  889.5 29.9 %while.58 = (s32[]{:T(128)}, f32[2048,64]{0,1:T(8,128)S(1)}, f32[2048,64]{0,1:T(8,128)S(1)}, f32[4,512,64]{1,2,0:T(8,128)}, s32[4]{0:T(128)S(1)}, /*index=5*/s32...) while((s32[]{:T(128)}, f32[2048,64]{0,1:T(8,128)S(1)}, ...), condition=%wide.region_15.15_spmd.clone, body=%wide.region_13.14_spmd.clone.sunk | while | flops 684197888 | bytes 35539192 | solution.py:113
  927.9 29.9 %while.58 = (s32[]{:T(128)}, f32[2048,64]{0,1:T(8,128)S(1)}, f32[2048,64]{0,1:T(8,128)S(1)}, f32[4,512,64]{1,2,0:T(8,128)}, s32[4]{0:T(128)S(1)}, /*index=5*/s32...) while((s32[]{:T(128)}, f32[2048,64]{0,1:T(8,128)S(1)}, ...), condition=%wide.region_15.15_spmd.clone, body=%wide.region_13.14_spmd.clone.sunk | while | flops 684197888 | bytes 35539192 | solution.py:113
  966.4 29.9 %while.58 = (s32[]{:T(128)}, f32[2048,64]{0,1:T(8,128)S(1)}, f32[2048,64]{0,1:T(8,128)S(1)}, f32[4,512,64]{1,2,0:T(8,128)}, s32[4]{0:T(128)S(1)}, /*index=5*/s32...) while((s32[]{:T(128)}, f32[2048,64]{0,1:T(8,128)S(1)}, ...), condition=%wide.region_15.15_spmd.clone, body=%wide.region_13.14_spmd.clone.sunk | while | flops 684197888 | bytes 35539192 | solution.py:113
  1034.6 58.2 %reduce-scatter.18.cloned.1.call-done = bf16[512,1024]{1,0:T(8,128)(2,1)} async-done(((bf16[2048,1024]{1,0:T(8,128)(2,1)}), bf16[512,1024]{1,0:T(8,128)(2,1)}) %reduce-scatter.18.cloned.1.call-update) | async-done | bytes 1048592 | tf_op jit(solution)/shard_map/reduce_scatter | solution.py:234
  1124.2 19.0 %reduce-scatter.20.cloned.1.call-done = f32[3,128,256]{1,2,0:T(8,128)} async-done(((f32[3,1024,256]{1,2,0:T(8,128)}), f32[3,128,256]{1,2,0:T(8,128)}) %reduce-scatter.20.cloned.1.call-update) | async-done | bytes 393232 | tf_op jit(solution)/shard_map/reduce_scatter | solution.py:248
  1145.1 77.2 %reduce-scatter.14.cloned.1.call-done = bf16[512,1024]{1,0:T(8,128)(2,1)} async-done(((bf16[2048,1024]{1,0:T(8,128)(2,1)}), bf16[512,1024]{1,0:T(8,128)(2,1)}) %reduce-scatter.14.cloned.1.call-update) | async-done | bytes 1048592 | tf_op jit(solution)/shard_map/reduce_scatter | solution.py:176
  1226.5 33.7 %reduce-scatter.28.cloned.1.call-done = f32[128,2]{1,0:T(8,128)} async-done(((f32[1024,2]{1,0:T(8,128)}), f32[128,2]{1,0:T(8,128)}) %reduce-scatter.28.cloned.1.call-update) | async-done | bytes 1040
  1273.3 35.7 %reduce-scatter.26.cloned.1.call-done = f32[704,128]{1,0:T(8,128)} async-done(((f32[704,1024]{1,0:T(8,128)}), f32[704,128]{1,0:T(8,128)}) %reduce-scatter.26.cloned.1.call-update) | async-done | bytes 360464 | tf_op jit(solution)/shard_map/reduce_scatter | solution.py:251
  1309.1 63.3 %reduce-scatter.24.cloned.1.call-done = f32[2,128,704]{1,2,0:T(8,128)} async-done(((f32[2,1024,704]{1,2,0:T(8,128)}), f32[2,128,704]{1,2,0:T(8,128)}) %reduce-scatter.24.cloned.1.call-update) | async-done | bytes 720912 | tf_op jit(solution)/shard_map/reduce_scatter | solution.py:250
  1372.4 39.6 %reduce-scatter.22.cloned.1.call-done = f32[256,128]{1,0:T(8,128)} async-done(((f32[256,1024]{1,0:T(8,128)}), f32[256,128]{1,0:T(8,128)}) %reduce-scatter.22.cloned.1.call-update) | async-done | bytes 131088 | tf_op jit(solution)/shard_map/reduce_scatter | solution.py:249
  (580 shorter events, 502.4 us)
Async XLA Ops:
  7.2 34.4 %all-gather.9.cloned.1.call-start = ((), (), s32[]{:S(2)}) async-start(), calls=%async_computation.10 | async-start | bytes 1769472 | tf_op jit(solution)/shard_map/all_gather | solution.py:135
  9.2 114.3 %all-gather.7.cloned.1.call-start = ((), (), s32[]{:S(2)}) async-start(), calls=%async_computation.9 | async-start | bytes 5242880 | tf_op jit(solution)/shard_map/all_gather | solution.py:146
  25.3 387.7 %reduce-scatter.12.cloned.1.call-start = ((), (), s32[]{:S(2)}) async-start(), calls=%async_computation.11 | async-start | bytes 10485760 | tf_op jit(solution)/shard_map/reduce_scatter | solution.py:160
  269.8 143.2 %copy-start.2 = (bf16[512,1024]{1,0:T(8,128)(2,1)S(1)}, bf16[512,1024]{1,0:T(8,128)(2,1)}, u32[]{:S(2)}) copy-start(bf16[512,1024]{1,0:T(8,128)(2,1)} %param.17) | copy-start | bytes 3145732
  269.8 277.2 %all-gather.13.cloned.1.call-start = ((), (), s32[]{:S(2)}) async-start(), calls=%async_computation.13 | async-start | bytes 3244032 | tf_op jit(solution)/shard_map/all_gather | solution.py:137
  271.7 143.3 %copy-start.19 = (f32[1,1024]{1,0:T(1,128)S(1)}, f32[1,1024]{1,0:T(1,128)}, u32[]{:S(2)}) copy-start(f32[1,1024]{1,0:T(1,128)} %get-tuple-element.425) | copy-start | bytes 12292
  271.7 289.3 %all-gather.11.cloned.1.call-start = ((), (), s32[]{:S(2)}) async-start(), calls=%async_computation.12 | async-start | bytes 5242880 | tf_op jit(solution)/shard_map/all_gather | solution.py:168
  414.9 342.4 %copy-start = (f32[512,1024]{1,0:T(8,128)}, f32[512,1024]{1,0:T(8,128)S(1)}, u32[]{:S(2)}) copy-start(f32[512,1024]{1,0:T(8,128)S(1)} %get-tuple-element.395) | copy-start | bytes 6291460
  415.0 342.4 %copy-start.23 = (f32[512]{0:T(512)}, f32[512]{0:T(512)S(1)}, u32[]{:S(2)}) copy-start(f32[512]{0:T(512)S(1)} %add_rsqrt_fusion) | copy-start | bytes 6148
  416.2 170.7 %all-gather.15.cloned.1.call-start = ((), (), s32[]{:S(2)}) async-start(), calls=%async_computation.14 | async-start | bytes 1622016 | tf_op jit(solution)/shard_map/all_gather | solution.py:138
  416.9 26.5 %collective-permute-start = (bf16[512,1024]{1,0:T(8,128)(2,1)S(1)}, bf16[512,1024]{1,0:T(8,128)(2,1)S(1)}, u32[]{:S(2)}, u32[]{:S(2)}) collective-permute-start(bf16[512,1024]{1,0:T(8,128)(2,1)S(1)} %copy-done.6), channel_id=1, source_target_pairs={{0,1},{1,2},{2,3},{3,0},{4,5},{5,6},{6,7},{7,4},{8,9},{9,10},{10,1... | collective-permute-start | bytes 3145736 | tf_op jit(solution)/shard_map/ppermute | solution.py:194
  444.5 36.6 %collective-permute-start.1 = (bf16[512,1024]{1,0:T(8,128)(2,1)S(1)}, bf16[512,1024]{1,0:T(8,128)(2,1)}, u32[]{:S(2)}, u32[]{:S(2)}) collective-permute-start(bf16[512,1024]{1,0:T(8,128)(2,1)S(1)} %collective-permute-done), channel_id=1, source_target_pairs={{0,1},{1,2},{2,3},{3,0},{4,5},{5,6},{6,7},{7,4},{8,9},{9,10},{10,1... | collective-permute-start | bytes 3145736 | tf_op jit(solution)/shard_map/ppermute | solution.py:194
  481.1 52.7 %collective-permute-start.2 = (bf16[512,1024]{1,0:T(8,128)(2,1)}, bf16[512,1024]{1,0:T(8,128)(2,1)}, u32[]{:S(2)}, u32[]{:S(2)}) collective-permute-start(bf16[512,1024]{1,0:T(8,128)(2,1)} %collective-permute-done.1), channel_id=1, source_target_pairs={{0,1},{1,2},{2,3},{3,0},{4,5},{5,6},{6,7},{7,4},{8,9},{9,10},{10,1... | collective-permute-start | bytes 3145736 | tf_op jit(solution)/shard_map/ppermute | solution.py:194
  491.5 262.9 %reduce-scatter.16.cloned.1.call-start = ((), (), s32[]{:S(2)}) async-start(), calls=%async_computation.16 | async-start | bytes 10485760 | tf_op jit(solution)/shard_map/reduce_scatter | solution.py:205
  609.8 230.9 %all-gather.17.cloned.1.call-start = ((), (), s32[]{:S(2)}) async-start(), calls=%async_computation.17 | async-start | bytes 5242880 | tf_op jit(solution)/shard_map/all_gather | solution.py:216
  759.0 333.8 %reduce-scatter.18.cloned.1.call-start = ((), (), s32[]{:S(2)}) async-start(), calls=%async_computation.18 | async-start | bytes 5242880 | tf_op jit(solution)/shard_map/reduce_scatter | solution.py:234
  846.1 153.7 %copy-start.10 = (f32[2048,32]{0,1:T(8,128)S(1)}, f32[2048,32]{0,1:T(8,128)}, u32[]{:S(2)}) copy-start(f32[2048,32]{0,1:T(8,128)} %copy-done.9) | copy-start | bytes 786436
  1017.4 125.8 %reduce-scatter.20.cloned.1.call-start = ((), (), s32[]{:S(2)}) async-start(), calls=%async_computation.19 | async-start | bytes 3538944 | tf_op jit(solution)/shard_map/reduce_scatter | solution.py:248
  1026.2 196.0 %reduce-scatter.14.cloned.1.call-start = ((), (), s32[]{:S(2)}) async-start(), calls=%async_computation.15 | async-start | bytes 5242880 | tf_op jit(solution)/shard_map/reduce_scatter | solution.py:176
  1034.5 225.7 %reduce-scatter.28.cloned.1.call-start = ((), (), s32[]{:S(2)}) async-start(), calls=%async_computation.23 | async-start | bytes 589824
  1095.9 213.1 %reduce-scatter.26.cloned.1.call-start = ((), (), s32[]{:S(2)}) async-start(), calls=%async_computation.22 | async-start | bytes 3244032 | tf_op jit(solution)/shard_map/reduce_scatter | solution.py:251
  1103.8 268.6 %reduce-scatter.24.cloned.1.call-start = ((), (), s32[]{:S(2)}) async-start(), calls=%async_computation.21 | async-start | bytes 6488064 | tf_op jit(solution)/shard_map/reduce_scatter | solution.py:250
  1115.4 296.6 %reduce-scatter.22.cloned.1.call-start = ((), (), s32[]{:S(2)}) async-start(), calls=%async_computation.20 | async-start | bytes 1179648 | tf_op jit(solution)/shard_map/reduce_scatter | solution.py:249
  1121.2 101.1 %copy-start.28 = (f32[512]{0:T(512)S(1)}, f32[512]{0:T(512)}, u32[]{:S(2)}) copy-start(f32[512]{0:T(512)} %copy-done.27) | copy-start | bytes 6148
  (28 other events, 831.1 us)
Sparse Core Ops, SparseCore 0:
  10.5 30.0 all-gather.8
  42.7 80.6 all-gather.6
  270.0 142.9 reduce-scatter.11
  415.3 32.3 all-gather.12
  449.7 111.3 all-gather.10
  563.4 23.5 all-gather.14
  609.9 144.4 reduce-scatter.15
  759.2 81.4 all-gather.16
  1017.5 75.2 reduce-scatter.17
  1096.4 46.7 reduce-scatter.19
  1145.5 76.7 reduce-scatter.13
  1225.5 34.6 reduce-scatter.27
  1264.2 44.8 reduce-scatter.25
  1313.3 59.0 reduce-scatter.23
  1376.0 35.9 reduce-scatter.21
